TPU v7x, 32 devices: a whole 2x2x4 slice. The times are simulated.
32 devices in a mesh: blk: 8 (over z, y), pix: 4 (over x, core).
Axes of the slice: x: 2, y: 2, z: 4, core: 2. Of those that a mesh axis runs over, the one named last changes fastest.
Arguments:
- images: bfloat16 [256, 16384], P('blk', 'pix'), may hold values from -14 to 14
- templates: bfloat16 [2304, 16384], P('blk', 'pix'), may hold values from -4 to 4
- routes: int32 [256, 4], P('blk'), may hold values from 0 to 7, all different within a row; in each aligned block of 32 rows (0 to 31, 32 to 63, ...) at most 24 rows name the same one
- image_weight: float32 [256], P('blk'), may hold values from 0.25 to 4
- template_weight: float32 [2304], P('blk'), may hold values from 0.25 to 4
Outputs:
- template_means: bfloat16 [2304, 16384], P('blk', 'pix')
- image_duals: float32 [256], P('blk')
Inputs may be any that keep to these rules, and one draw needn't show every extreme that they name: `routes`: each image names 4 different template blocks. Among the 32 images of one block, at most 24 name any one template block, and some template block is named by exactly 24 of them. Every template block is named by some image.
All inputs are finite; a program needn't handle non-finite values.
Results may differ from a plain program's by a relative error of at most 0.0046.
Values may be sent and summed in bfloat16 or wider, within the bound.
A program may use at most 64 MiB of HBM per device.

v0:
```python
import jax
import jax.numpy as jnp
from jax import lax
from jax.sharding import PartitionSpec as P

SWEEPS = 2


def on_device(images, templates, routes, image_weight, template_weight):
    blocks = lax.axis_size("blk")
    img_dev = images.shape[0]
    admits = routes.shape[1]
    capacity = max(2, (3 * img_dev * admits + 2 * blocks - 1) // (2 * blocks))
    target = routes.reshape(-1)
    target_hot = (target[:, None] == jnp.arange(blocks, dtype=jnp.int32)[None, :]).astype(jnp.int32)
    before = jnp.cumsum(target_hot, axis=0) - target_hot
    position = jnp.sum(before * target_hot, axis=1)
    slot_of = target * capacity + position
    wanted = jnp.arange(blocks * capacity, dtype=jnp.int32)
    matches = slot_of[None, :] == wanted[:, None]
    filled = jnp.any(matches, axis=1)
    owner_image = jnp.sum(
        jnp.where(matches, jnp.arange(target.shape[0], dtype=jnp.int32)[None, :] // admits, 0),
        axis=1,
    )
    outgoing = jnp.where(filled[:, None], images[owner_image], jnp.zeros((), images.dtype))
    outgoing = outgoing.reshape(blocks, capacity, images.shape[1])
    slot_flags = filled.astype(jnp.bfloat16).reshape(blocks, capacity)
    template_log = jnp.log(template_weight)
    arrived_piece = lax.all_to_all(outgoing, "blk", split_axis=0, concat_axis=0, tiled=True)
    marks_piece = lax.all_to_all(slot_flags, "blk", split_axis=0, concat_axis=0, tiled=True)
    partial_value = jnp.einsum(
        "bmp,tp->bmt", arrived_piece, templates, preferred_element_type=jnp.float32
    )
    summed = lax.psum(partial_value, "pix")
    usable = marks_piece > 0
    image_log = jnp.log(image_weight)
    slot_duals = jnp.zeros((blocks, capacity), jnp.float32)
    image_duals = jnp.zeros((img_dev,), jnp.float32)
    for sweep_index in range(SWEEPS):
        column_terms = jnp.where(usable[:, :, None], summed + slot_duals[:, :, None], -jnp.inf)
        column_peak = jnp.max(column_terms, axis=(0, 1))
        template_duals = (
            template_log
            - column_peak
            - jnp.log(jnp.sum(jnp.exp(column_terms - column_peak), axis=(0, 1)))
        )
        row_terms = summed + template_duals
        row_peak = jnp.max(row_terms, axis=2)
        row_total = jnp.sum(jnp.exp(row_terms - row_peak[:, :, None]), axis=2)
        levels = row_peak + jnp.log(row_total)
        back_levels = lax.all_to_all(levels, "blk", split_axis=0, concat_axis=0, tiled=True)
        level_routes = back_levels.reshape(-1)[slot_of].reshape(img_dev, admits)
        route_peak = jnp.max(level_routes, axis=1)
        image_duals = (
            image_log
            - route_peak
            - jnp.log(jnp.sum(jnp.exp(level_routes - route_peak[:, None]), axis=1))
        )
        duals_send = jnp.where(filled, image_duals[owner_image], 0.0).reshape(blocks, capacity)
        slot_duals = lax.all_to_all(duals_send, "blk", split_axis=0, concat_axis=0, tiled=True)
    column_terms = jnp.where(usable[:, :, None], summed + slot_duals[:, :, None], -jnp.inf)
    column_peak = jnp.max(column_terms, axis=(0, 1))
    column_exp = jnp.exp(column_terms - column_peak)
    plan_weights = (column_exp / jnp.sum(column_exp, axis=(0, 1))).astype(jnp.bfloat16)
    template_means = jnp.einsum(
        "bmt,bmp->tp", plan_weights, arrived_piece, preferred_element_type=jnp.float32
    ).astype(jnp.bfloat16)
    return (template_means, image_duals)


def solution(mesh):
    in_specs = (P("blk", "pix"), P("blk", "pix"), P("blk", None), P("blk"), P("blk"))
    out_specs = (P("blk", "pix"), P("blk"))
    return jax.shard_map(
        on_device, mesh=mesh, in_specs=in_specs, out_specs=out_specs, check_vma=False
    )
```

profile of v0, /device:TPU:0, one launch (start us, length us, event | category | flops | bytes accessed | tf_op | source)
XLA Modules:
  0.0 203.8 jit_solution(13468316568536961378)
XLA Ops:
  7.2 0.9 copy.17
  9.0 2.7 %gather_fusion = bf16[192,4096]{1,0:T(8,128)(2,1)} fusion(bf16[32,4096]{1,0:T(8,128)(2,1)S(1)} %copy-done.1, s32[1024]{0:T(1024)S(1)} %pad_clamp_fusion.1), kind=kCustom, calls=%fused_computation | custom fusion | bytes 3146496 | tf_op jit(solution)/shard_map/gather | solution.py:26
  11.7 2.7 %broadcast_select_fusion = bf16[8,24,4096]{2,1,0:T(8,128)(2,1)} fusion(bf16[8,24,4096]{2,1,0:T(8,128)(2,1)} %bitcast.88, pred[8,24]{1,0:T(8,128)(4,1)S(1)} %broadcast_in_dim.77), kind=kLoop, calls=%fused_computation.7 | loop fusion | flops 786432 | bytes 3145920 | tf_op jit(solution)/shard_map/jit(_where)/select_n | solution.py:26
  14.4 7.4 %all-to-all-start.1 = ((bf16[8,24,4096]{2,1,0:T(8,128)(2,1)}), bf16[8,24,4096]{2,1,0:T(8,128)(2,1)}, u32[]{:S(2)}, u32[]{:S(2)}) async-start(bf16[8,24,4096]{2,1,0:T(8,128)(2,1)} %broadcast_select_fusion), calls=%async_computation.1 | async-start | bytes 3145728 | tf_op jit(solution)/shard_map/all_to_all | solution.py:30
  22.1 0.7 reshape.347
  22.8 36.2 %all-to-all-done.1 = bf16[8,24,4096]{2,1,0:T(8,128)(2,1)} async-done(((bf16[8,24,4096]{2,1,0:T(8,128)(2,1)}), bf16[8,24,4096]{2,1,0:T(8,128)(2,1)}, u32[]{:S(2)}, u32[]{:S(2)}) %all-to-all-start.1) | async-done | bytes 1572896 | tf_op jit(solution)/shard_map/all_to_all | solution.py:30
  59.0 3.6 %all-to-all-start = ((bf16[8,1,24]{2,1,0:T(2,128)(2,1)}), bf16[8,1,24]{2,1,0:T(2,128)(2,1)S(1)}, u32[]{:S(2)}, u32[]{:S(2)}) async-start(bf16[8,1,24]{2,1,0:T(2,128)(2,1)} %reshape.347), calls=%async_computation | async-start | bytes 8192 | tf_op jit(solution)/shard_map/all_to_all | solution.py:31
  62.7 3.3 %fusion.1 = f32[8,24,288]{2,1,0:T(8,128)} fusion(bf16[8,24,4096]{2,1,0:T(8,128)(2,1)} %all-to-all-done.1, bf16[288,4096]{1,0:T(8,128)(2,1)S(1)} %copy-done), kind=kOutput, calls=%fused_computation.5 | convolution fusion | flops 452984832 | bytes 4153344 | tf_op jit(solution)/shard_map/bmp,tp->bmt/dot_general | solution.py:32
  66.0 3.1 %all-to-all-done = bf16[8,1,24]{2,1,0:T(2,128)(2,1)S(1)} async-done(((bf16[8,1,24]{2,1,0:T(2,128)(2,1)}), bf16[8,1,24]{2,1,0:T(2,128)(2,1)S(1)}, u32[]{:S(2)}, u32[]{:S(2)}) %all-to-all-start) | async-done | bytes 416 | tf_op jit(solution)/shard_map/all_to_all | solution.py:31
  69.1 31.1 %all-reduce.2.cloned.1.call-done = f32[8,24,288]{2,1,0:T(8,128)} async-done(((f32[8,24,288]{2,1,0:T(8,128)}), f32[8,24,288]{2,1,0:T(8,128)}) %all-reduce.2.cloned.1.call-update) | async-done | bytes 221200 | tf_op jit(solution)/shard_map/psum | solution.py:35
  100.2 1.1 select_reduce_fusion
  101.3 1.1 exponential_reduce_fusion.3
  102.5 1.1 add_reduce_fusion.1
  103.5 1.2 exponential_reduce_fusion.2
  104.7 0.6 log_add_fusion.1
  105.3 5.5 %all-to-all-start.2 = ((f32[8,1,24]{2,1,0:T(1,128)}), f32[8,1,24]{2,1,0:T(1,128)S(1)}, u32[]{:S(2)}, u32[]{:S(2)}) async-start(f32[8,1,24]{2,1,0:T(1,128)} %bitcast.5), calls=%async_computation.2 | async-start | bytes 8192 | tf_op jit(solution)/shard_map/all_to_all | solution.py:52
  110.8 6.4 %all-to-all-done.2 = f32[8,1,24]{2,1,0:T(1,128)S(1)} async-done(((f32[8,1,24]{2,1,0:T(1,128)}), f32[8,1,24]{2,1,0:T(1,128)S(1)}, u32[]{:S(2)}, u32[]{:S(2)}) %all-to-all-start.2) | async-done | bytes 800 | tf_op jit(solution)/shard_map/all_to_all | solution.py:52
  117.2 0.5 broadcast.505
  117.7 0.7 reduce.6
  118.5 1.3 gather_fusion.1
  120.2 0.7 fusion.18
  120.9 0.7 fusion.17
  121.6 19.9 %select_select_fusion.1 = f32[192]{0:T(256)S(1)} fusion(pred[192]{0:T(512)(128)(4,1)S(1)} %fusion.11, f32[]{:T(128)} %bitcast.8, f32[]{:T(128)} %bitcast.9, f32[]{:T(128)} %bitcast.10, f32[]{:T(128)} %bitcast.11, f32[]{:T(128)} %bitcast.12, f32[]{:T(128)} %bitcast.13, f32[]{:T(128)} %bitcast.14, f32[]{:T(128)} %bitcast.15, f32[]{:T(128)} %bitcast.16, ...), kind=kLoop, calls=%fused_computation.46 | loop fusion | flops 12096 | bytes 1856 | tf_op jit(solution)/shard_map/jit(_where)/select_n | solution.py:60
  141.6 8.8 %all_to_all.35 = f32[8,1,24]{2,1,0:T(1,128)S(1)} all-to-all(f32[8,1,24]{2,1,0:T(1,128)S(1)} %select_n.88), channel_id=1, replica_groups=mesh['blk'=8,'pix'=4] {'blk'}, dimensions={0} | all-to-all | bytes 1536 | tf_op jit(solution)/shard_map/all_to_all | solution.py:61
  151.1 8.9 %all_to_all.36 = f32[8,1,24]{2,1,0:T(1,128)S(1)} all-to-all(f32[8,1,24]{2,1,0:T(1,128)S(1)} %bitcast.97), channel_id=1, replica_groups=mesh['blk'=8,'pix'=4] {'blk'}, dimensions={0} | all-to-all | bytes 1536 | tf_op jit(solution)/shard_map/all_to_all | solution.py:52
  159.9 0.7 reduce.7
  160.7 1.3 gather_fusion.2
  162.4 0.7 fusion.16
  163.1 0.7 fusion.15
  163.8 20.1 %select_select_fusion = f32[192]{0:T(256)S(1)} fusion(pred[192]{0:T(512)(128)(4,1)S(1)} %fusion.11, f32[]{:T(128)} %bitcast.42, f32[]{:T(128)} %bitcast.43, f32[]{:T(128)} %bitcast.44, f32[]{:T(128)} %bitcast.45, f32[]{:T(128)} %bitcast.46, f32[]{:T(128)} %bitcast.47, f32[]{:T(128)} %bitcast.48, f32[]{:T(128)} %bitcast.49, f32[]{:T(128)} %bitcast.50, ...), kind=kLoop, calls=%fused_computation.45 | loop fusion | flops 12096 | bytes 1856 | tf_op jit(solution)/shard_map/jit(_where)/select_n | solution.py:60
  184.0 8.8 %all_to_all.37 = f32[8,1,24]{2,1,0:T(1,128)S(1)} all-to-all(f32[8,1,24]{2,1,0:T(1,128)S(1)} %select_n.91), channel_id=1, replica_groups=mesh['blk'=8,'pix'=4] {'blk'}, dimensions={0} | all-to-all | bytes 1536 | tf_op jit(solution)/shard_map/all_to_all | solution.py:61
  193.2 3.7 %fusion = bf16[288,4096]{1,0:T(8,128)(2,1)} fusion(bf16[8,24,4096]{2,1,0:T(8,128)(2,1)} %all-to-all-done.1, f32[8,24,288]{2,1,0:T(8,128)S(1)} %copy-done.2, f32[288]{0:T(512)S(1)} %fusion.5, f32[288]{0:T(512)S(1)} %fusion.4, f32[8,24]{1,0:T(8,128)S(1)} %bitcast.91, pred[8,24]{1,0:T(8,128)(4,1)S(1)} %compare_bitcast_fusion), kind=kOutput, calls=%fused_computation.4 | convolution fusion | flops 454440960 | bytes 4156608 | tf_op jit(solution)/shard_map/bmt,bmp->tp/dot_general | solution.py:66
  (54 shorter events, 3.2 us)
Async XLA Ops:
  7.2 55.5 %copy-start = (bf16[288,4096]{1,0:T(8,128)(2,1)S(1)}, bf16[288,4096]{1,0:T(8,128)(2,1)}, u32[]{:S(2)}) copy-start(bf16[288,4096]{1,0:T(8,128)(2,1)} %param.6) | copy-start | bytes 7077892
  7.2 1.8 copy-start.1
  14.4 7.5 %copy-start.4 = (s32[32,4]{0,1:T(4,128)S(1)}, s32[32,4]{0,1:T(4,128)}, u32[]{:S(2)}) copy-start(s32[32,4]{0,1:T(4,128)} %param.7) | copy-start | bytes 1540
  14.4 44.5 %all-to-all-start.1 = ((bf16[8,24,4096]{2,1,0:T(8,128)(2,1)}), bf16[8,24,4096]{2,1,0:T(8,128)(2,1)}, u32[]{:S(2)}, u32[]{:S(2)}) async-start(bf16[8,24,4096]{2,1,0:T(8,128)(2,1)} %broadcast_select_fusion), calls=%async_computation.1 | async-start | bytes 3145728 | tf_op jit(solution)/shard_map/all_to_all | solution.py:30
  59.0 10.1 %all-to-all-start = ((bf16[8,1,24]{2,1,0:T(2,128)(2,1)}), bf16[8,1,24]{2,1,0:T(2,128)(2,1)S(1)}, u32[]{:S(2)}, u32[]{:S(2)}) async-start(bf16[8,1,24]{2,1,0:T(2,128)(2,1)} %reshape.347), calls=%async_computation | async-start | bytes 8192 | tf_op jit(solution)/shard_map/all_to_all | solution.py:31
  62.6 39.8 %copy-start.5 = (f32[288]{0:T(512)S(1)}, f32[288]{0:T(512)}, u32[]{:S(2)}) copy-start(f32[288]{0:T(512)} %param.9) | copy-start | bytes 3460
  62.6 37.6 %all-reduce.2.cloned.1.call-start = ((), (), s32[]{:S(2)}) async-start(), calls=%async_computation.6 | async-start | bytes 589824 | tf_op jit(solution)/shard_map/psum | solution.py:35
  66.0 54.2 %copy-start.6 = (f32[32]{0:T(128)S(1)}, f32[32]{0:T(128)}, u32[]{:S(2)}) copy-start(f32[32]{0:T(128)} %param.8) | copy-start | bytes 388
  100.2 50.3 %copy-start.2 = (f32[8,24,288]{2,1,0:T(8,128)S(1)}, f32[8,24,288]{2,1,0:T(8,128)}, u32[]{:S(2)}) copy-start(f32[8,24,288]{2,1,0:T(8,128)} %all-reduce.2.cloned.1.call-done) | copy-start | bytes 663556
  105.3 11.9 %all-to-all-start.2 = ((f32[8,1,24]{2,1,0:T(1,128)}), f32[8,1,24]{2,1,0:T(1,128)S(1)}, u32[]{:S(2)}, u32[]{:S(2)}) async-start(f32[8,1,24]{2,1,0:T(1,128)} %bitcast.5), calls=%async_computation.2 | async-start | bytes 8192 | tf_op jit(solution)/shard_map/all_to_all | solution.py:52
  162.4 34.5 %copy-start.3 = (f32[32]{0:T(128)}, f32[32]{0:T(128)S(1)}, u32[]{:S(2)}) copy-start(f32[32]{0:T(128)S(1)} %log_subtract_fusion.2) | copy-start | bytes 388
Sparse Core Ops, SparseCore 0:
  66.3 33.7 all-reduce.1
where the time goes:
time: 205 us; the launch traced here: 204 us
  waiting for transfers between devices  76.8 us (37%)
  other arithmetic  51.3 us (25%)
  blocking collectives  26.6 us (13%)
  starting transfers between devices  16.6 us (8%)
  between operations  14.3 us (7%)
  local copies, waits for them, and re-layouts  11.1 us (5%)
  matrix products  7.05 us (3%)
    select_n x2, other arithmetic, on_device(): jnp.where(filled, image_duals[owner_image], 0.0).reshape(blocks, capacity)  40 us
    all_to_all x1, waiting for transfers between devices, on_device(): lax.all_to_all(outgoing, 'blk', split_axis=0, concat_axis=0, tiled=True)  36.2 us
    psum x1, waiting for transfers between devices, on_device(): summed = lax.psum(partial_value, 'pix')  31.1 us
    all_to_all x2, blocking collectives, on_device(): lax.all_to_all(duals_send, 'blk', split_axis=0, concat_axis=0, tiled=True)  17.7 us
    all_to_all x1, blocking collectives, on_device(): lax.all_to_all(levels, 'blk', split_axis=0, concat_axis=0, tiled=True)  8.86 us
    all_to_all x1, starting transfers between devices, on_device(): lax.all_to_all(outgoing, 'blk', split_axis=0, concat_axis=0, tiled=True)  7.44 us
    all_to_all x1, waiting for transfers between devices, on_device(): lax.all_to_all(levels, 'blk', split_axis=0, concat_axis=0, tiled=True)  6.41 us
    all_to_all x1, starting transfers between devices, on_device(): lax.all_to_all(levels, 'blk', split_axis=0, concat_axis=0, tiled=True)  5.52 us
  transfers between devices with their start and end apart: 4, of which 4 were waited for; matrix products, arithmetic and copies ran while one was open for 2% of the time, Pallas kernels for 0%

commit v1 on v0

--- a/solution.py
+++ b/solution.py
@@ -2,6 +2,7 @@
 import jax.numpy as jnp
 from jax import lax
 from jax.sharding import PartitionSpec as P
+from jax.lax import all_gather
 
 SWEEPS = 2
 
@@ -32,7 +33,13 @@
     partial_value = jnp.einsum(
         "bmp,tp->bmt", arrived_piece, templates, preferred_element_type=jnp.float32
     )
-    summed = lax.psum(partial_value, "pix")
+
+    def sides_reach(local_array):
+        opened = all_gather(local_array, "pix")
+        newest = jnp.sum(opened, 0)
+        return newest
+
+    summed = sides_reach(partial_value)
     usable = marks_piece > 0
     image_log = jnp.log(image_weight)
     slot_duals = jnp.zeros((blocks, capacity), jnp.float32)

time: 205 us -> 166 us (0.81)
  waiting for transfers between devices: 76.8 us -> 43.6 us
  between operations: 14.3 us -> 0.94 us
  blocking collectives: 26.6 us -> 37.7 us
  other arithmetic: 51.3 us -> 49 us
    psum x1 -> x0, waiting for transfers between devices: 31.1 us -> none  [on_device(): summed = lax.psum(partial_value, 'pix')]
    all_gather x0 -> x1, blocking collectives: none -> 11.2 us  [sides_reach(): opened = all_gather(local_array, 'pix')]
    all_to_all x1, starting transfers between devices: 3.64 us -> 7.31 us  [on_device(): lax.all_to_all(slot_flags, 'blk', split_axis=0, concat_axis=0, tiled=True)]
    all_to_all x1, waiting for transfers between devices: 3.09 us -> 0.86 us  [on_device(): lax.all_to_all(slot_flags, 'blk', split_axis=0, concat_axis=0, tiled=True)]
    all_to_all x1, starting transfers between devices: 7.44 us -> 5.27 us  [on_device(): lax.all_to_all(outgoing, 'blk', split_axis=0, concat_axis=0, tiled=True)]
  transfers between devices with their start and end apart: 4 -> 3, of which waited for: 4 -> 3; matrix products, arithmetic and copies ran while one was open for 2% -> 4% of each run, Pallas kernels for 0% -> 0%
where the time goes in v1:
time: 166 us; the launch traced here: 165 us
  other arithmetic  49 us (30%)
  waiting for transfers between devices  43.6 us (26%)
  blocking collectives  37.7 us (23%)
  starting transfers between devices  16.2 us (10%)
  local copies, waits for them, and re-layouts  11.1 us (7%)
  matrix products  6.33 us (4%)
    select_n x2, other arithmetic, on_device(): jnp.where(filled, image_duals[owner_image], 0.0).reshape(blocks, capacity)  40.2 us
    all_to_all x1, waiting for transfers between devices, on_device(): lax.all_to_all(outgoing, 'blk', split_axis=0, concat_axis=0, tiled=True)  36.3 us
    all_to_all x2, blocking collectives, on_device(): lax.all_to_all(duals_send, 'blk', split_axis=0, concat_axis=0, tiled=True)  17.7 us
    all_gather x1, blocking collectives, sides_reach(): opened = all_gather(local_array, 'pix')  11.2 us
    all_to_all x1, blocking collectives, on_device(): lax.all_to_all(levels, 'blk', split_axis=0, concat_axis=0, tiled=True)  8.86 us
    all_to_all x1, starting transfers between devices, on_device(): lax.all_to_all(slot_flags, 'blk', split_axis=0, concat_axis=0, tiled=True)  7.31 us
    all_to_all x1, waiting for transfers between devices, on_device(): lax.all_to_all(levels, 'blk', split_axis=0, concat_axis=0, tiled=True)  6.41 us
    all_to_all x1, starting transfers between devices, on_device(): lax.all_to_all(outgoing, 'blk', split_axis=0, concat_axis=0, tiled=True)  5.27 us
  transfers between devices with their start and end apart: 3, of which 3 were waited for; matrix products, arithmetic and copies ran while one was open for 4% of the time, Pallas kernels for 0%

profile of v1, /device:TPU:0, one launch (start us, length us, event | category | flops | bytes accessed | tf_op | source)
XLA Modules:
  0.0 165.0 jit_solution(6401863094919313721)
XLA Ops:
  0.7 0.9 copy.17
  2.3 0.7 reshape.348
  3.0 7.3 %all-to-all-start = ((bf16[8,1,24]{2,1,0:T(2,128)(2,1)}), bf16[8,1,24]{2,1,0:T(2,128)(2,1)S(1)}, u32[]{:S(2)}, u32[]{:S(2)}) async-start(bf16[8,1,24]{2,1,0:T(2,128)(2,1)} %reshape.348), calls=%async_computation | async-start | bytes 8192 | tf_op jit(solution)/shard_map/all_to_all | solution.py:32
  10.5 2.7 %gather_fusion = bf16[192,4096]{1,0:T(8,128)(2,1)} fusion(bf16[32,4096]{1,0:T(8,128)(2,1)S(1)} %copy-done.1, s32[1024]{0:T(1024)S(1)} %pad_clamp_fusion.1), kind=kCustom, calls=%fused_computation | custom fusion | bytes 3146496 | tf_op jit(solution)/shard_map/gather | solution.py:27
  13.2 2.7 %broadcast_select_fusion = bf16[8,24,4096]{2,1,0:T(8,128)(2,1)} fusion(bf16[8,24,4096]{2,1,0:T(8,128)(2,1)} %bitcast.89, pred[8,24]{1,0:T(8,128)(4,1)S(1)} %broadcast_in_dim.77), kind=kLoop, calls=%fused_computation.7 | loop fusion | flops 786432 | bytes 3145920 | tf_op jit(solution)/shard_map/jit(_where)/select_n | solution.py:27
  15.9 0.9 all-to-all-done
  16.8 5.3 %all-to-all-start.1 = ((bf16[8,24,4096]{2,1,0:T(8,128)(2,1)}), bf16[8,24,4096]{2,1,0:T(8,128)(2,1)}, u32[]{:S(2)}, u32[]{:S(2)}) async-start(bf16[8,24,4096]{2,1,0:T(8,128)(2,1)} %broadcast_select_fusion), calls=%async_computation.1 | async-start | bytes 3145728 | tf_op jit(solution)/shard_map/all_to_all | solution.py:31
  22.3 36.3 %all-to-all-done.1 = bf16[8,24,4096]{2,1,0:T(8,128)(2,1)} async-done(((bf16[8,24,4096]{2,1,0:T(8,128)(2,1)}), bf16[8,24,4096]{2,1,0:T(8,128)(2,1)}, u32[]{:S(2)}, u32[]{:S(2)}) %all-to-all-start.1) | async-done | bytes 1572896 | tf_op jit(solution)/shard_map/all_to_all | solution.py:31
  58.6 2.6 %fusion.1 = f32[8,24,288]{2,1,0:T(8,128)S(1)} fusion(bf16[8,24,4096]{2,1,0:T(8,128)(2,1)} %all-to-all-done.1, bf16[288,4096]{1,0:T(8,128)(2,1)S(1)} %copy-done), kind=kOutput, calls=%fused_computation.5 | convolution fusion | flops 452984832 | bytes 4153344 | tf_op jit(solution)/shard_map/bmp,tp->bmt/dot_general | solution.py:33
  61.2 11.2 %all-gather = f32[32,24,288]{2,1,0:T(8,128)} all-gather(f32[8,24,288]{2,1,0:T(8,128)S(1)} %fusion.1), channel_id=2, replica_groups=mesh['blk'=8,'pix'=4] {'pix'}, dimensions={0}, use_global_device_ids=true | all-gather | bytes 1105920 | tf_op jit(solution)/shard_map/all_gather | solution.py:38
  72.4 1.4 reduce_sum.97
  74.2 0.2 exponential_reduce_fusion.2
  74.4 0.6 log_add_fusion.1
  75.0 3.6 %all-to-all-start.2 = ((f32[8,1,24]{2,1,0:T(1,128)}), f32[8,1,24]{2,1,0:T(1,128)S(1)}, u32[]{:S(2)}, u32[]{:S(2)}) async-start(f32[8,1,24]{2,1,0:T(1,128)} %bitcast.6), calls=%async_computation.2 | async-start | bytes 8192 | tf_op jit(solution)/shard_map/all_to_all | solution.py:59
  78.6 6.4 %all-to-all-done.2 = f32[8,1,24]{2,1,0:T(1,128)S(1)} async-done(((f32[8,1,24]{2,1,0:T(1,128)}), f32[8,1,24]{2,1,0:T(1,128)S(1)}, u32[]{:S(2)}, u32[]{:S(2)}) %all-to-all-start.2) | async-done | bytes 800 | tf_op jit(solution)/shard_map/all_to_all | solution.py:59
  85.0 0.5 broadcast.505
  85.5 0.7 reduce.6
  86.3 1.3 gather_fusion.1
  88.0 0.7 fusion.18
  88.7 0.7 fusion.17
  89.4 20.1 %select_select_fusion.1 = f32[192]{0:T(256)S(1)} fusion(pred[192]{0:T(512)(128)(4,1)S(1)} %fusion.11, f32[]{:T(128)} %bitcast.9, f32[]{:T(128)} %bitcast.10, f32[]{:T(128)} %bitcast.11, f32[]{:T(128)} %bitcast.12, f32[]{:T(128)} %bitcast.13, f32[]{:T(128)} %bitcast.14, f32[]{:T(128)} %bitcast.15, f32[]{:T(128)} %bitcast.16, f32[]{:T(128)} %bitcast.17, ...), kind=kLoop, calls=%fused_computation.46 | loop fusion | flops 12096 | bytes 1856 | tf_op jit(solution)/shard_map/jit(_where)/select_n | solution.py:67
  109.6 8.8 %all_to_all.35 = f32[8,1,24]{2,1,0:T(1,128)S(1)} all-to-all(f32[8,1,24]{2,1,0:T(1,128)S(1)} %select_n.88), channel_id=1, replica_groups=mesh['blk'=8,'pix'=4] {'blk'}, dimensions={0} | all-to-all | bytes 1536 | tf_op jit(solution)/shard_map/all_to_all | solution.py:68
  118.9 0.2 exponential_reduce_fusion
  119.1 8.9 %all_to_all.36 = f32[8,1,24]{2,1,0:T(1,128)S(1)} all-to-all(f32[8,1,24]{2,1,0:T(1,128)S(1)} %bitcast.99), channel_id=1, replica_groups=mesh['blk'=8,'pix'=4] {'blk'}, dimensions={0} | all-to-all | bytes 1536 | tf_op jit(solution)/shard_map/all_to_all | solution.py:59
  128.0 0.7 reduce.7
  128.7 1.3 gather_fusion.2
  130.2 0.2 exponential_reduce_fusion.4
  130.4 0.7 fusion.16
  131.2 0.7 fusion.15
  131.9 20.1 %select_select_fusion = f32[192]{0:T(256)S(1)} fusion(pred[192]{0:T(512)(128)(4,1)S(1)} %fusion.11, f32[]{:T(128)} %bitcast.43, f32[]{:T(128)} %bitcast.44, f32[]{:T(128)} %bitcast.45, f32[]{:T(128)} %bitcast.46, f32[]{:T(128)} %bitcast.47, f32[]{:T(128)} %bitcast.48, f32[]{:T(128)} %bitcast.49, f32[]{:T(128)} %bitcast.50, f32[]{:T(128)} %bitcast.51, ...), kind=kLoop, calls=%fused_computation.45 | loop fusion | flops 12096 | bytes 1856 | tf_op jit(solution)/shard_map/jit(_where)/select_n | solution.py:67
  152.1 8.8 %all_to_all.37 = f32[8,1,24]{2,1,0:T(1,128)S(1)} all-to-all(f32[8,1,24]{2,1,0:T(1,128)S(1)} %select_n.91), channel_id=1, replica_groups=mesh['blk'=8,'pix'=4] {'blk'}, dimensions={0} | all-to-all | bytes 1536 | tf_op jit(solution)/shard_map/all_to_all | solution.py:68
  161.2 3.7 %fusion = bf16[288,4096]{1,0:T(8,128)(2,1)} fusion(bf16[8,24,4096]{2,1,0:T(8,128)(2,1)} %all-to-all-done.1, f32[8,24,288]{2,1,0:T(8,128)S(1)} %reduce_sum.97, f32[288]{0:T(512)S(1)} %fusion.5, f32[288]{0:T(512)S(1)} %fusion.4, f32[8,24]{1,0:T(8,128)S(1)} %bitcast.93, pred[8,24]{1,0:T(8,128)(4,1)S(1)} %compare_bitcast_fusion), kind=kOutput, calls=%fused_computation.4 | convolution fusion | flops 454440960 | bytes 4156608 | tf_op jit(solution)/shard_map/bmt,bmp->tp/dot_general | solution.py:73
  (51 shorter events, 3.1 us)
Async XLA Ops:
  0.6 58.0 %copy-start = (bf16[288,4096]{1,0:T(8,128)(2,1)S(1)}, bf16[288,4096]{1,0:T(8,128)(2,1)}, u32[]{:S(2)}) copy-start(bf16[288,4096]{1,0:T(8,128)(2,1)} %param.6) | copy-start | bytes 7077892
  0.6 9.9 %copy-start.1 = (bf16[32,4096]{1,0:T(8,128)(2,1)S(1)}, bf16[32,4096]{1,0:T(8,128)(2,1)}, u32[]{:S(2)}) copy-start(bf16[32,4096]{1,0:T(8,128)(2,1)} %param.5) | copy-start | bytes 786436
  3.0 13.8 %all-to-all-start = ((bf16[8,1,24]{2,1,0:T(2,128)(2,1)}), bf16[8,1,24]{2,1,0:T(2,128)(2,1)S(1)}, u32[]{:S(2)}, u32[]{:S(2)}) async-start(bf16[8,1,24]{2,1,0:T(2,128)(2,1)} %reshape.348), calls=%async_computation | async-start | bytes 8192 | tf_op jit(solution)/shard_map/all_to_all | solution.py:32
  15.9 6.1 %copy-start.3 = (s32[32,4]{0,1:T(4,128)S(1)}, s32[32,4]{0,1:T(4,128)}, u32[]{:S(2)}) copy-start(s32[32,4]{0,1:T(4,128)} %param.7) | copy-start | bytes 1540
  16.8 41.8 %all-to-all-start.1 = ((bf16[8,24,4096]{2,1,0:T(8,128)(2,1)}), bf16[8,24,4096]{2,1,0:T(8,128)(2,1)}, u32[]{:S(2)}, u32[]{:S(2)}) async-start(bf16[8,24,4096]{2,1,0:T(8,128)(2,1)} %broadcast_select_fusion), calls=%async_computation.1 | async-start | bytes 3145728 | tf_op jit(solution)/shard_map/all_to_all | solution.py:31
  61.2 12.8 %copy-start.4 = (f32[288]{0:T(512)S(1)}, f32[288]{0:T(512)}, u32[]{:S(2)}) copy-start(f32[288]{0:T(512)} %param.9) | copy-start | bytes 3460
  72.4 15.6 %copy-start.5 = (f32[32]{0:T(128)S(1)}, f32[32]{0:T(128)}, u32[]{:S(2)}) copy-start(f32[32]{0:T(128)} %param.8) | copy-start | bytes 388
  75.0 10.1 %all-to-all-start.2 = ((f32[8,1,24]{2,1,0:T(1,128)}), f32[8,1,24]{2,1,0:T(1,128)S(1)}, u32[]{:S(2)}, u32[]{:S(2)}) async-start(f32[8,1,24]{2,1,0:T(1,128)} %bitcast.6), calls=%async_computation.2 | async-start | bytes 8192 | tf_op jit(solution)/shard_map/all_to_all | solution.py:59
  130.4 34.5 %copy-start.2 = (f32[32]{0:T(128)}, f32[32]{0:T(128)S(1)}, u32[]{:S(2)}) copy-start(f32[32]{0:T(128)S(1)} %log_subtract_fusion.2) | copy-start | bytes 388
